TPU v7x, 128 devices: a whole 4x4x4 slice. The times are simulated.
128 devices in a mesh: fsdp: 16 (over x, y), dp: 8 (over z, core).
Axes of the slice: x: 4, y: 4, z: 4, core: 2. Of those that a mesh axis runs over, the one named last changes fastest.
Arguments:
- tokens: bfloat16 [32768, 960], P(('fsdp', 'dp')), may hold values from -6 to 6
- layer_weights: bfloat16 [1, 960, 10240], P(None, None, ('fsdp', 'dp'))
- norm_gains: bfloat16 [1, 1920], P(None, ('fsdp', 'dp')), may hold values from 0.5 to 1.5
- seq_ids: int32 [32768], P(('fsdp', 'dp')), may hold values from 0 to 255, as said below
- out_grad: bfloat16 [32768, 960], P(('fsdp', 'dp')), may hold values from -6 to 6
Outputs:
- activations: bfloat16 [32768, 960], P(('fsdp', 'dp'))
- input_grad: float32 [32768, 960], P(('fsdp', 'dp'))
- weight_grad: float32 [1, 960, 10240], P(None, None, ('fsdp', 'dp'))
- gain_grad: float32 [1, 1920], P(None, ('fsdp', 'dp'))
Inputs may be any that keep to these rules, and one draw needn't show every extreme that they name: `seq_ids`: within each device's 256 rows: 0 in the first row, never falling, rising by at most one from a row to the next, so every sequence lies whole on one device; on some device all rows form one sequence, on another every row is a sequence of its own.
All inputs are finite; a program needn't handle non-finite values.
Results may differ from a plain program's by a relative error of at most 0.013.
Values may be sent and summed in bfloat16 or wider, within the bound.
A program may use at most 256 MiB of HBM per device.

v0:
```python
import jax
import jax.numpy as jnp
from jax import lax
from jax.sharding import PartitionSpec as P

QUERY_HEADS = 15
KEY_VALUE_HEADS = 5
HEAD_SIZE = 64
epsilon = 1e-05
rope_base = 100000.0


def mix_heads(pattern, left, right):
    return jnp.einsum(pattern, left, right, preferred_element_type=jnp.float32)


def across(left, right):
    return lax.dot_general(
        left, right, (((0,), (0,)), ((), ())), preferred_element_type=jnp.float32
    )


def against(left, right):
    return lax.dot_general(
        left, right, (((1,), (1,)), ((), ())), preferred_element_type=jnp.float32
    )


def tables(block_ids, head_width):
    sequence_length = block_ids.shape[0]
    row_index = jnp.arange(sequence_length, dtype=jnp.int32)
    same_seq = block_ids[:, None] == block_ids[None, :]
    seq_start = jnp.min(jnp.where(same_seq, row_index[None, :], sequence_length), axis=1)
    position = (row_index - seq_start).astype(jnp.float32)
    inv_freq = rope_base ** (-jnp.arange(0, head_width, 2).astype(jnp.float32) / head_width)
    angles = position[:, None] * inv_freq[None, :]
    allowed = same_seq & (row_index[None, :] <= row_index[:, None])
    return (jnp.cos(angles)[:, None, :], jnp.sin(angles)[:, None, :], allowed)


def apply_rotary(values, cosine_table, sine_table, direction):
    half_dim = values.shape[-1] // 2
    a = values[..., :half_dim]
    b = values[..., half_dim:]
    return jnp.concatenate(
        [
            a * cosine_table - direction * b * sine_table,
            b * cosine_table + direction * a * sine_table,
        ],
        axis=-1,
    )


def norm_forward(values, gain):
    inv_rms = lax.rsqrt(jnp.mean(values * values, axis=-1, keepdims=True) + epsilon)
    return (inv_rms, (values * inv_rms * gain).astype(jnp.bfloat16))


def norm_backward(d_norm, values, inv_rms, gain):
    u = d_norm * gain
    d_gain = jnp.sum(d_norm * values * inv_rms, axis=0)
    d_values = inv_rms * u - values * inv_rms**3 * jnp.mean(u * values, axis=-1, keepdims=True)
    return (d_values, d_gain)


def widths(weight_tree, cosine_table):
    head_width = cosine_table.shape[-1] * 2
    query_width = QUERY_HEADS * head_width
    key_value_width = KEY_VALUE_HEADS * head_width
    perceptron_begin = 2 * query_width + 2 * key_value_width
    hidden_width = (weight_tree.shape[1] - perceptron_begin) // 3
    return (head_width, query_width, key_value_width, perceptron_begin, hidden_width)


def scores(query_rows, key_rows, allowed, head_width):
    score_vals = mix_heads("tkgd,skd->kgts", query_rows, key_rows) * head_width ** (-0.5)
    return jnp.where(allowed, score_vals, -1e30)


def layer_forward(stream, weight_tree, gain_row, cosine_table, sine_table, allowed):
    head_width, query_width, key_value_width, perceptron_begin, hidden_width = widths(
        weight_tree, cosine_table
    )
    width = stream.shape[1]
    sequence_length = stream.shape[0]
    head_group = QUERY_HEADS // KEY_VALUE_HEADS
    gain_a = gain_row[:width].astype(jnp.float32)
    gain_b = gain_row[width:].astype(jnp.float32)
    rms_a, normed_a = norm_forward(stream, gain_a)
    query_key_value = jnp.dot(
        normed_a,
        weight_tree[:, : query_width + 2 * key_value_width],
        preferred_element_type=jnp.float32,
    )
    query_rows = (
        apply_rotary(
            query_key_value[:, :query_width].reshape(sequence_length, QUERY_HEADS, head_width),
            cosine_table,
            sine_table,
            1.0,
        )
        .astype(jnp.bfloat16)
        .reshape(sequence_length, KEY_VALUE_HEADS, head_group, head_width)
    )
    key_rows = apply_rotary(
        query_key_value[:, query_width : query_width + key_value_width].reshape(
            sequence_length, KEY_VALUE_HEADS, head_width
        ),
        cosine_table,
        sine_table,
        1.0,
    ).astype(jnp.bfloat16)
    value_rows = (
        query_key_value[:, query_width + key_value_width : query_width + 2 * key_value_width]
        .reshape(sequence_length, KEY_VALUE_HEADS, head_width)
        .astype(jnp.bfloat16)
    )
    score_vals = scores(query_rows, key_rows, allowed, head_width)
    row_max = jnp.max(score_vals, axis=-1, keepdims=True)
    expon = jnp.exp(score_vals - row_max)
    row_sum = jnp.sum(expon, axis=-1, keepdims=True)
    log_total = row_max + jnp.log(row_sum)
    attended = (
        mix_heads("kgts,skd->tkgd", (expon / row_sum).astype(jnp.bfloat16), value_rows)
        .reshape(sequence_length, query_width)
        .astype(jnp.bfloat16)
    )
    middle = stream + against(
        attended, weight_tree[:, query_width + 2 * key_value_width : perceptron_begin]
    )
    rms_b, normed_b = norm_forward(middle, gain_b)
    gate_up = jnp.dot(
        normed_b,
        weight_tree[:, perceptron_begin : perceptron_begin + 2 * hidden_width],
        preferred_element_type=jnp.float32,
    )
    gate_val = gate_up[:, :hidden_width]
    upward = gate_up[:, hidden_width:]
    hidden = (jax.nn.silu(gate_val) * upward).astype(jnp.bfloat16)
    result = middle + against(hidden, weight_tree[:, perceptron_begin + 2 * hidden_width :])
    return (
        result,
        (
            stream,
            rms_a,
            normed_a,
            query_rows,
            key_rows,
            value_rows,
            log_total,
            attended,
            middle,
            rms_b,
            normed_b,
            gate_val,
            upward,
            hidden,
        ),
    )


def layer_backward(upstream, saved_acts, weight_tree, gain_row, cosine_table, sine_table, allowed):
    (
        stream,
        rms_a,
        normed_a,
        query_rows,
        key_rows,
        value_rows,
        log_total,
        attended,
        middle,
        rms_b,
        normed_b,
        gate_val,
        upward,
        hidden,
    ) = saved_acts
    head_width, query_width, key_value_width, perceptron_begin, hidden_width = widths(
        weight_tree, cosine_table
    )
    width = stream.shape[1]
    sequence_length = stream.shape[0]
    head_group = QUERY_HEADS // KEY_VALUE_HEADS
    gain_a = gain_row[:width].astype(jnp.float32)
    gain_b = gain_row[width:].astype(jnp.float32)
    out_rounded = upstream.astype(jnp.bfloat16)
    d_hidden = jnp.dot(
        out_rounded,
        weight_tree[:, perceptron_begin + 2 * hidden_width :],
        preferred_element_type=jnp.float32,
    )
    d_down = across(out_rounded, hidden)
    sig_gate = jax.nn.sigmoid(gate_val)
    d_gate = d_hidden * upward * sig_gate * (1.0 + gate_val * (1.0 - sig_gate))
    d_upward = d_hidden * gate_val * sig_gate
    d_gate_up = jnp.concatenate([d_gate, d_upward], axis=1).astype(jnp.bfloat16)
    d_normed_b = against(
        d_gate_up, weight_tree[:, perceptron_begin : perceptron_begin + 2 * hidden_width]
    )
    d_gate_up_w = across(normed_b, d_gate_up)
    d_mid_norm, d_gain_b = norm_backward(d_normed_b, middle, rms_b, gain_b)
    d_middle = upstream + d_mid_norm
    middle_cast = d_middle.astype(jnp.bfloat16)
    attended_gradient = (
        jnp.dot(
            middle_cast,
            weight_tree[:, query_width + 2 * key_value_width : perceptron_begin],
            preferred_element_type=jnp.float32,
        )
        .astype(jnp.bfloat16)
        .reshape(sequence_length, KEY_VALUE_HEADS, head_group, head_width)
    )
    d_out_w = across(middle_cast, attended)
    expon = jnp.exp(scores(query_rows, key_rows, allowed, head_width) - log_total)
    d_v = mix_heads("kgts,tkgd->skd", expon.astype(jnp.bfloat16), attended_gradient)
    d_p = mix_heads("tkgd,skd->kgts", attended_gradient, value_rows)
    d_s = expon * (d_p - jnp.sum(expon * d_p, axis=-1, keepdims=True))
    d_s_rounded = (d_s * head_width ** (-0.5)).astype(jnp.bfloat16)
    d_q = mix_heads("kgts,skd->tkgd", d_s_rounded, key_rows).reshape(
        sequence_length, QUERY_HEADS, head_width
    )
    d_k = mix_heads("kgts,tkgd->skd", d_s_rounded, query_rows)
    d_q = apply_rotary(d_q, cosine_table, sine_table, -1.0).reshape(sequence_length, query_width)
    d_k = apply_rotary(d_k, cosine_table, sine_table, -1.0).reshape(
        sequence_length, key_value_width
    )
    d_qkv = jnp.concatenate(
        [d_q, d_k, d_v.reshape(sequence_length, key_value_width)], axis=1
    ).astype(jnp.bfloat16)
    d_normed_a = against(d_qkv, weight_tree[:, : query_width + 2 * key_value_width])
    d_qkv_w = across(normed_a, d_qkv)
    d_in_norm, d_gain_a = norm_backward(d_normed_a, stream, rms_a, gain_a)
    d_stream = d_middle + d_in_norm
    weight_part = jnp.concatenate([d_qkv_w, d_out_w, d_gate_up_w, d_down], axis=1)
    return (d_stream, weight_part, jnp.concatenate([d_gain_a, d_gain_b]))


def body(tokens, layer_weights, norm_gains, seq_ids, out_grad):
    layer_count = layer_weights.shape[0]
    cosine_table, sine_table, allowed = tables(seq_ids, HEAD_SIZE)
    stream = tokens.astype(jnp.float32)
    held_list = []
    layer = 0
    gathered = lax.all_gather(layer_weights[layer], ("fsdp", "dp"), axis=1, tiled=True)
    gain_row = lax.all_gather(norm_gains[layer], ("fsdp", "dp"), axis=0, tiled=True)
    held_list.append((gathered, gain_row))
    stream, saved_acts = layer_forward(
        stream, gathered, gain_row, cosine_table, sine_table, allowed
    )
    saved_list = [saved_acts]
    upstream = out_grad.astype(jnp.float32)
    weight_parts = [None] * layer_count
    gain_parts = [None] * layer_count
    for layer in reversed(range(layer_count)):
        gathered, gain_row = (
            lax.all_gather(layer_weights[layer], ("fsdp", "dp"), axis=1, tiled=True),
            lax.all_gather(norm_gains[layer], ("fsdp", "dp"), axis=0, tiled=True),
        )
        upstream, weight_term, gain_term = layer_backward(
            upstream, saved_list[layer], gathered, gain_row, cosine_table, sine_table, allowed
        )
        weight_parts[layer], gain_parts[layer] = (
            lax.psum_scatter(weight_term, ("fsdp", "dp"), scatter_dimension=1, tiled=True),
            lax.psum_scatter(gain_term, ("fsdp", "dp"), scatter_dimension=0, tiled=True),
        )
    weight_grad = jnp.stack(weight_parts)
    gain_grad = jnp.stack(gain_parts)
    return (stream.astype(jnp.bfloat16), upstream, weight_grad, gain_grad)


def solution(mesh):
    return jax.shard_map(
        body,
        mesh=mesh,
        in_specs=(
            P(("fsdp", "dp"), None),
            P(None, None, ("fsdp", "dp")),
            P(None, ("fsdp", "dp")),
            P(("fsdp", "dp")),
            P(("fsdp", "dp"), None),
        ),
        out_specs=(
            P(("fsdp", "dp"), None),
            P(("fsdp", "dp"), None),
            P(None, None, ("fsdp", "dp")),
            P(None, ("fsdp", "dp")),
        ),
        check_vma=False,
    )
```

profile of v0, /device:TPU:0, one launch (start us, length us, event | category | flops | bytes accessed | tf_op | source)
XLA Modules:
  0.0 977.7 jit_solution(9443763462687554647)
XLA Ops:
  7.2 0.7 all-gather.4.cloned.1.call-update
  8.0 0.9 dynamic-update-slice
  8.8 68.9 %all-reduce = bf16[1920]{0:T(1024)(128)(2,1)S(1)} all-reduce(bf16[1920]{0:T(1024)(128)(2,1)S(1)} %dynamic-update-slice), channel_id=2, replica_groups=mesh['fsdp'=16,'dp'=8] {'fsdp','dp'}, use_global_device_ids=true, to_apply=%add | all-reduce | flops 1920 | bytes 7680
  77.8 0.9 fusion.59
  78.7 1.2 fusion.49
  80.0 0.9 compare_and_fusion
  81.0 19.9 %all-gather.4.cloned.1.call-done = bf16[1,960,10240]{1,2,0:T(8,128)(2,1)} async-done(((bf16[1,960,80]{1,2,0:T(8,128)(2,1)}), bf16[1,960,10240]{1,2,0:T(8,128)(2,1)}) %all-gather.4.cloned.1.call-update) | async-done | bytes 19660816 | tf_op jit(solution)/shard_map/all_gather | solution.py:245
  100.9 3.1 fusion.16
  104.5 0.8 fusion.76
  105.9 0.8 fusion.38
  107.2 2.5 multiply_reduce_fusion.2
  109.7 9.5 fusion.3
  119.3 8.5 multiply_convert_fusion.1
  127.7 8.7 multiply_reduce_fusion
  136.7 2.2 fusion.39
  139.0 2.6 fusion.77
  141.6 0.7 fusion.46
  142.3 8.1 fusion.42
  150.5 8.2 fusion.23
  158.7 3.8 fusion.60
  162.5 8.2 fusion.29
  170.9 5.2 convolution_bitcast_fusion
  176.1 3.8 fusion.58
  179.9 41.2 %concatenate.43 = f32[960,10240]{1,0:T(8,128)} concatenate(f32[960,1600]{1,0:T(8,128)} %fusion.58, f32[960,960]{1,0:T(8,128)} %fusion.60, f32[960,5120]{1,0:T(8,128)} %fusion.29, f32[960,2560]{1,0:T(8,128)} %convolution_bitcast_fusion), dimensions={1} | concatenate | bytes 78643200 | tf_op jit(solution)/shard_map/concatenate | solution.py:235
  221.1 40.9 %copy.27 = f32[960,10240]{0,1:T(8,128)} copy(f32[960,10240]{1,0:T(8,128)} %concatenate.43) | data formatting | bytes 78643200
  262.0 4.4 fusion.57
  266.5 70.4 %all-reduce.1 = f32[1920]{0:T(1024)S(1)} all-reduce(f32[1920]{0:T(1024)S(1)} %pad_maximum_fusion.11), channel_id=5, replica_groups=mesh['fsdp'=16,'dp'=8] {'fsdp','dp'}, use_global_device_ids=true, to_apply=%region_11.12.clone | all-reduce | flops 1920 | bytes 15360
  337.5 2.4 fusion.54
  339.9 5.8 fusion.35
  345.7 623.0 %reduce-scatter.4.cloned.1.call-done = f32[80,960]{1,0:T(8,128)} async-done(((f32[10240,960]{1,0:T(8,128)}), f32[80,960]{1,0:T(8,128)}) %reduce-scatter.4.cloned.1.call-update) | async-done | bytes 307216
  968.7 1.2 copy.28
  969.9 0.9 copy.18
  (59 shorter events, 3.1 us)
Async XLA Ops:
  7.2 93.8 %all-gather.4.cloned.1.call-start = ((), (), s32[]{:S(2)}) async-start(), calls=%async_computation.1 | async-start | bytes 21135360 | tf_op jit(solution)/shard_map/all_gather | solution.py:245
  7.9 960.8 %reduce-scatter.4.cloned.1.call-start = ((), (), s32[]{:S(2)}) async-start(), calls=%async_computation.2 | async-start | bytes 42270720
  104.4 1.4 copy-start.11
  104.4 1.4 copy-start.12
  104.4 1.4 copy-start.14
  105.2 36.3 %copy-start = (f32[5,3,256,256]{2,3,1,0:T(8,128)}, f32[5,3,256,256]{2,3,1,0:T(8,128)S(1)}, u32[]{:S(2)}) copy-start(f32[5,3,256,256]{2,3,1,0:T(8,128)S(1)} %get-tuple-element.37) | copy-start | bytes 11796484
  105.8 1.4 copy-start.1
  106.6 3.1 copy-start.9
  109.7 9.5 copy-start.2
  127.7 8.7 copy-start.3
  127.7 8.7 copy-start.5
  142.3 8.2 copy-start.13
  158.7 3.8 copy-start.4
  158.7 3.8 copy-start.6
  162.5 8.2 copy-start.10
  162.5 8.3 copy-start.8
  162.5 8.4 copy-start.7
  262.0 4.4 copy-start.15
Sparse Core Ops, SparseCore 0:
  11.0 89.9 all-gather.3
  262.1 706.5 reduce-scatter.3
where the time goes:
time: 980 us; the launch traced here: 978 us
  waiting for transfers between devices  644 us (66%)
  blocking collectives  139 us (14%)
  matrix products  86.9 us (9%)
  local copies, waits for them, and re-layouts  86.4 us (9%)
  between operations  14.3 us (1%)
    unnamed x3, waiting for transfers between devices  624 us
    unnamed x2, blocking collectives  139 us
    unnamed x38, local copies, waits for them, and re-layouts  44.5 us
    concatenate x1, local copies, waits for them, and re-layouts, layer_backward(): jnp.concatenate([d_qkv_w, d_out_w, d_gate_up_w, d_down], axis=1)  41.2 us
    dot_general x4, matrix products, against(): lax.dot_general(left, right, (((1,), (1,)), ((), ())), preferred_element_...  21.4 us
    dot_general x6, matrix products, mix_heads(): return jnp.einsum(pattern, left, right, preferred_element_type=jnp.float32)  21.3 us
    dot_general x4, matrix products, across(): lax.dot_general(left, right, (((0,), (0,)), ((), ())), preferred_element_...  20.9 us
    all_gather x1, waiting for transfers between devices, body(): lax.all_gather(layer_weights[layer], ('fsdp', 'dp'), axis=1, tiled=True)  19.9 us
  transfers between devices with their start and end apart: 2, of which 2 were waited for; matrix products, arithmetic and copies ran while one was open for 2% of the time, Pallas kernels for 0%

commit v1 on v0

--- a/solution.py
+++ b/solution.py
@@ -242,7 +242,12 @@
     stream = tokens.astype(jnp.float32)
     held_list = []
     layer = 0
-    gathered = lax.all_gather(layer_weights[layer], ("fsdp", "dp"), axis=1, tiled=True)
+    gathered = jnp.concatenate(
+        lax.all_to_all(
+            jnp.stack([layer_weights[layer]] * lax.axis_size(("fsdp", "dp"))), ("fsdp", "dp"), 0, 0
+        ),
+        axis=1,
+    )
     gain_row = lax.all_gather(norm_gains[layer], ("fsdp", "dp"), axis=0, tiled=True)
     held_list.append((gathered, gain_row))
     stream, saved_acts = layer_forward(

time: 980 us -> 1300 us (1.33)
  blocking collectives: 139 us -> 466 us
  waiting for transfers between devices: 644 us -> 624 us
    unnamed x2, blocking collectives: 139 us -> 466 us
    all_gather x1, waiting for transfers between devices: 19.9 us -> 0.01 us  [body(): lax.all_gather(layer_weights[layer], ('fsdp', 'dp'), axis=1, tiled=True)]
  transfers between devices with their start and end apart: 2 -> 3, of which waited for: 2 -> 1; matrix products, arithmetic and copies ran while one was open for 2% -> 3% of each run, Pallas kernels for 0% -> 0%
where the time goes in v1:
time: 1300 us
  waiting for transfers between devices  624 us (48%)
  blocking collectives  466 us (36%)
  local copies, waits for them, and re-layouts  93.7 us (7%)
  matrix products  86.6 us (7%)
  between operations  14.4 us (1%)
    unnamed x3, waiting for transfers between devices  624 us
    unnamed x2, blocking collectives  466 us
    unnamed x38, local copies, waits for them, and re-layouts  43.8 us
    concatenate x1, local copies, waits for them, and re-layouts, layer_backward(): jnp.concatenate([d_qkv_w, d_out_w, d_gate_up_w, d_down], axis=1)  41.2 us
  transfers between devices with their start and end apart: 3, of which 1 were waited for; matrix products, arithmetic and copies ran while one was open for 3% of the time, Pallas kernels for 0%

profile of v1, /device:TPU:0, one launch (start us, length us, event | category | flops | bytes accessed | tf_op | source)
XLA Modules:
  0.0 1301.2 jit_solution(12796143470656602817)
XLA Ops:
  7.2 0.7 all-gather.4.cloned.1.call-update
  7.9 8.0 stack.9
  15.9 11.6 all-to-all-start
  27.9 396.8 %all-reduce = bf16[1920]{0:T(1024)(128)(2,1)S(1)} all-reduce(bf16[1920]{0:T(1024)(128)(2,1)S(1)} %dynamic-update-slice), channel_id=2, replica_groups=mesh['fsdp'=16,'dp'=8] {'fsdp','dp'}, use_global_device_ids=true, to_apply=%add | all-reduce | flops 1920 | bytes 7680
  425.4 3.1 fusion.15
  428.9 0.8 fusion.76
  429.6 0.6 fusion.12
  430.2 0.8 fusion.38
  431.0 0.5 copy-done
  431.6 2.6 multiply_reduce_fusion.2
  434.3 9.5 fusion.3
  443.8 8.5 multiply_convert_fusion.1
  452.3 8.1 multiply_reduce_fusion
  460.7 2.4 fusion.39
  463.1 2.6 fusion.77
  465.7 0.7 fusion.46
  466.5 8.2 fusion.42
  474.7 8.2 fusion.27
  482.9 3.8 fusion.60
  486.7 8.2 fusion.29
  495.1 5.2 convolution_bitcast_fusion
  500.3 3.8 fusion.58
  504.1 41.2 %concatenate.43 = f32[960,10240]{1,0:T(8,128)} concatenate(f32[960,1600]{1,0:T(8,128)} %fusion.58, f32[960,960]{1,0:T(8,128)} %fusion.60, f32[960,5120]{1,0:T(8,128)} %fusion.29, f32[960,2560]{1,0:T(8,128)} %convolution_bitcast_fusion), dimensions={1} | concatenate | bytes 78643200 | tf_op jit(solution)/shard_map/concatenate | solution.py:235
  545.3 40.9 %copy.33 = f32[960,10240]{0,1:T(8,128)} copy(f32[960,10240]{1,0:T(8,128)} %concatenate.43) | data formatting | bytes 78643200
  586.2 4.4 fusion.57
  590.7 69.2 %all-reduce.1 = f32[1920]{0:T(1024)S(1)} all-reduce(f32[1920]{0:T(1024)S(1)} %pad_maximum_fusion.11), channel_id=5, replica_groups=mesh['fsdp'=16,'dp'=8] {'fsdp','dp'}, use_global_device_ids=true, to_apply=%region_11.12.clone | all-reduce | flops 1920 | bytes 15360
  659.9 0.6 dynamic-slice_bitcast_fusion
  660.5 2.4 fusion.54
  662.9 5.8 fusion.35
  668.7 623.6 %reduce-scatter.4.cloned.1.call-done = f32[80,960]{1,0:T(8,128)} async-done(((f32[10240,960]{1,0:T(8,128)}), f32[80,960]{1,0:T(8,128)}) %reduce-scatter.4.cloned.1.call-update) | async-done | bytes 307216
  1292.3 1.2 copy.34
  1293.5 0.9 copy.24
  (62 shorter events, 2.0 us)
Async XLA Ops:
  7.2 436.7 %all-gather.4.cloned.1.call-start = ((), (), s32[]{:S(2)}) async-start(), calls=%async_computation.2 | async-start | bytes 21135360 | tf_op jit(solution)/shard_map/all_gather | solution.py:262
  15.9 11.7 copy-start.15
  15.9 408.8 %copy-start.14 = (s32[256]{0:T(256)S(1)}, s32[256]{0:T(256)}, u32[]{:S(2)}) copy-start(s32[256]{0:T(256)} %param.8) | copy-start | bytes 3076
  15.9 409.0 %copy-start.2 = (bf16[256,960]{0,1:T(8,128)(2,1)S(1)}, bf16[256,960]{0,1:T(8,128)(2,1)}, u32[]{:S(2)}) copy-start(bf16[256,960]{0,1:T(8,128)(2,1)} %param.5) | copy-start | bytes 1474564
  15.9 409.5 %all-to-all-start = ((bf16[128,960,80]{1,2,0:T(8,128)(2,1)}), bf16[128,960,80]{1,2,0:T(8,128)(2,1)}, u32[]{:S(2)}, u32[]{:S(2)}) async-start(bf16[128,960,80]{1,2,0:T(8,128)(2,1)} %stack.9), calls=%async_computation | async-start | bytes 41943040 | tf_op jit(solution)/shard_map/all_to_all | solution.py:246
  27.5 1264.8 %reduce-scatter.4.cloned.1.call-start = ((), (), s32[]{:S(2)}) async-start(), calls=%async_computation.3 | async-start | bytes 42270720
  428.8 1.4 copy-start.12
  428.8 1.4 copy-start.13
  429.6 2.0 copy-start
  431.6 2.7 copy-start.10
  434.3 9.5 copy-start.3
  452.3 8.2 copy-start.4
  452.3 8.2 copy-start.6
  460.7 5.0 copy-start.1
  482.9 3.8 copy-start.5
  482.9 3.8 copy-start.7
  486.7 8.2 copy-start.11
  486.7 8.3 copy-start.9
  486.7 8.4 copy-start.8
Sparse Core Ops, SparseCore 0:
  11.0 351.8 all-gather.3
  586.3 705.9 reduce-scatter.3
